TPU v7x, 128 devices: a whole 4x4x4 slice. The times are simulated.
128 devices in a mesh: occ: 8 (over x, core), vir: 16 (over y, z).
Axes of the slice: x: 4, y: 4, z: 4, core: 2. Of those that a mesh axis runs over, the one named last changes fastest.
Arguments:
- amplitudes: bfloat16 [8, 2, 4096, 4096], P('occ', None, None, 'vir'), may hold values from -6 to 6
- coulomb: bfloat16 [8, 2, 4096, 4096], P('occ', None, None, 'vir'), may hold values from -6 to 6
- ladder_tiles: bfloat16 [256, 128, 128], P('vir'), may hold values from -0.1875 to 0.1875
- cycle_tiles: bfloat16 [256, 128, 128], P('vir'), may hold values from -0.25 to 0.25
- ladder_screen: int32 [32, 8], replicated, may hold values from 0 to 31, as said below
- tile_slot: int32 [256], replicated, may hold values from 0 to 255, each once
- cycle_screen: int32 [64, 4], replicated, may hold values from 0 to 63, as said below
- cycle_rows: int32 [32, 48], replicated, may hold values from 0 to 63, as said below
- cycle_count: int32 [32], replicated, may hold values from 1 to 48, 1024 in all
- slab_occ: int32 [8], replicated, may hold values from 0 to 399
- window_occ: int32 [2], replicated, may hold values from 0 to 399
- occ_energy: float32 [400], replicated, may hold values from -3 to -0.5
- vir_energy: float32 [4096], replicated, may hold values from 0.4 to 4
Outputs:
- updated: bfloat16 [8, 2, 4096, 4096], P('occ', None, None, 'vir')
Inputs may be any that keep to these rules, and one draw needn't show every extreme that they name: `ladder_screen`: each row names 8 different tiles. `cycle_screen`: each row names 4 different row tiles. `cycle_rows`: each row names 48 different block columns; the first cycle_count of them are used. `cycle_count`: the counts sum to exactly 1024, and the largest is exactly 48.
All inputs are finite; a program needn't handle non-finite values.
Results may differ from a plain program's by a relative error of at most 0.003.
Values may be sent and summed in bfloat16 or wider, within the bound.
No kernel may reach another device: no remote copies, remote signals or barrier semaphores. Data moves between devices by JAX's collectives and lax.ppermute only.
A program may use at most 192 MiB of HBM per device.

v0:
```python
import math
import jax
import jax.numpy as jnp
from jax import lax
from jax.sharding import PartitionSpec as P


def body(
    amplitudes,
    coulomb,
    ladder_tiles,
    cycle_tiles,
    ladder_screen,
    tile_slot,
    cycle_screen,
    cycle_rows,
    cycle_count,
    slab_occ,
    window_occ,
    occ_energy,
    vir_energy,
):
    occ_count = lax.axis_size("occ")
    vir_count = lax.axis_size("vir")
    dev_count = occ_count * vir_count
    slab_rows, window, width_all, block_cols = amplitudes.shape
    tile_side = ladder_tiles.shape[1]
    tile_count = width_all // tile_side
    ladder_keep = ladder_screen.shape[1]
    cycle_keep = cycle_screen.shape[1]
    column_tiles = cycle_screen.shape[0]
    rows_here = width_all // dev_count
    slab_all = slab_rows * occ_count
    all_ladder, all_cycle = (
        lax.all_gather(ladder_tiles, "vir", axis=0, tiled=True),
        lax.all_gather(cycle_tiles, "vir", axis=0, tiled=True),
    )
    front, inner = (1, rows_here)
    split = amplitudes.reshape(slab_rows, window, front, occ_count, vir_count, inner, block_cols)
    flat = split.reshape(1, slab_rows, window, front, dev_count, inner, block_cols)
    moved = lax.all_to_all(flat, ("occ", "vir"), split_axis=4, concat_axis=0, tiled=True)
    moved = moved.reshape(occ_count, vir_count, slab_rows, window, front, inner, block_cols)
    moved = moved.transpose(0, 2, 3, 4, 5, 1, 6)
    cycle_amp = moved.reshape(slab_all, window, front * inner, width_all)
    extent = slab_rows * window * block_cols
    arranged = amplitudes.transpose(2, 0, 1, 3).reshape(tile_count, tile_side, extent)
    slots = tile_slot.reshape(tile_count, ladder_keep)
    group = math.gcd(tile_count, 8)

    def ladder_block(start):
        screen_part = lax.dynamic_slice_in_dim(ladder_screen, start, group, 0)
        slot_part = lax.dynamic_slice_in_dim(slots, start, group, 0)
        picked_rows = arranged[screen_part]
        weights = all_ladder[slot_part]
        return jnp.einsum(
            "akrc,akce->are", weights, picked_rows, preferred_element_type=jnp.float32
        )

    starts = jnp.arange(0, tile_count, group, dtype=jnp.int32)
    total = lax.map(ladder_block, starts)
    ladder = total.reshape(width_all, slab_rows, window, block_cols).transpose(1, 2, 0, 3)
    source = cycle_amp.reshape(slab_all, window, front, inner, tile_count, tile_side)
    source = source.transpose(1, 4, 2, 0, 3, 5).reshape(
        window * tile_count, front, slab_all * inner, tile_side
    )
    cycle_sel = all_cycle.reshape(column_tiles, cycle_keep, tile_side, tile_side)
    device = lax.axis_index("occ") * vir_count + lax.axis_index("vir")
    my_tile = device * rows_here // tile_side
    columns = lax.dynamic_index_in_dim(cycle_rows, my_tile, 0, keepdims=False)
    used = lax.dynamic_index_in_dim(cycle_count, my_tile, 0, keepdims=False)
    valid = jnp.arange(columns.shape[0], dtype=jnp.int32) < used
    picked = source[cycle_screen[columns], 0]
    part = jnp.einsum(
        "emrc,emcb->erb", picked, cycle_sel[columns], preferred_element_type=jnp.float32
    )
    part = jnp.where(valid[:, None, None], part, 0.0)
    placed = (
        jnp.zeros((column_tiles, slab_all * inner, tile_side), jnp.float32).at[columns].add(part)
    )
    cycle_cols = placed.reshape(column_tiles, front, slab_all * inner, tile_side)
    cycle_cols = cycle_cols.astype(jnp.bfloat16).reshape(
        window, tile_count, front, slab_all, inner, tile_side
    )
    cycle_view = cycle_cols.transpose(3, 0, 2, 4, 1, 5).reshape(
        slab_all, window, front * inner, width_all
    )
    shaped = cycle_view.reshape(occ_count, slab_rows, window, front, inner, vir_count, block_cols)
    shaped = shaped.transpose(0, 5, 1, 2, 3, 4, 6).reshape(
        dev_count, slab_rows, window, front, 1, inner, block_cols
    )
    back = lax.all_to_all(shaped, ("occ", "vir"), split_axis=0, concat_axis=4, tiled=True)
    cycle = back.reshape(slab_rows, window, width_all, block_cols)
    occ_total = occ_energy.shape[0]
    orbital_ids = jnp.arange(occ_total, dtype=jnp.int32)
    my_slab = lax.dynamic_slice_in_dim(slab_occ, lax.axis_index("occ") * slab_rows, slab_rows)
    energy_i = jnp.sum(
        jnp.where(my_slab[:, None] == orbital_ids[None, :], occ_energy[None, :], 0.0), axis=1
    )
    energy_j = jnp.sum(
        jnp.where(window_occ[:, None] == orbital_ids[None, :], occ_energy[None, :], 0.0), axis=1
    )
    energy_b = lax.dynamic_slice_in_dim(vir_energy, lax.axis_index("vir") * block_cols, block_cols)
    denominator = (
        vir_energy[None, None, :, None]
        + energy_b[None, None, None, :]
        - energy_i[:, None, None, None]
        - energy_j[None, :, None, None]
    )
    value = coulomb.astype(jnp.float32) + ladder + cycle.astype(jnp.float32)
    return (value / denominator).astype(jnp.bfloat16)


def solution(mesh):
    return jax.shard_map(
        body,
        mesh=mesh,
        in_specs=(
            P("occ", None, None, "vir"),
            P("occ", None, None, "vir"),
            P("vir", None, None),
            P("vir", None, None),
            P(),
            P(),
            P(),
            P(),
            P(),
            P(),
            P(),
            P(),
            P(),
        ),
        out_specs=P("occ", None, None, "vir"),
        check_vma=False,
    )
```

profile of v0, /device:TPU:1, one launch (start us, length us, event | category | flops | bytes accessed | tf_op | source)
XLA Modules:
  0.0 347.0 jit_solution(11415876466510590525)
XLA Ops:
  8.0 4.8 %copy.67 = bf16[1,1,2,1,128,32,256]{6,5,2,3,1,0,4:T(8,128)(2,1)} copy(bf16[1,1,2,1,128,32,256]{6,5,4,2,3,1,0:T(8,128)(2,1)} %bitcast.87) | data formatting | bytes 8388608 | tf_op jit(solution)/shard_map/reshape;reshape | solution.py:40
  12.9 11.9 %all-to-all-start = ((bf16[1,1,2,1,128,32,256]{6,5,2,3,1,0,4:T(8,128)(2,1)}), bf16[1,1,2,1,128,32,256]{6,5,2,3,1,0,4:T(8,128)(2,1)}, u32[]{:S(2)}, u32[]{:S(2)}) async-start(bf16[1,1,2,1,128,32,256]{6,5,2,3,1,0,4:T(8,128)(2,1)} %copy.67), calls=%async_computation | async-start | bytes 8388608 | tf_op jit(solution)/shard_map/all_to_all | solution.py:41
  27.1 10.1 %copy.64 = bf16[4096,1,2,256]{3,2,0,1:T(2,128)(2,1)} copy(bf16[4096,1,2,256]{3,0,2,1:T(8,128)(2,1)} %bitcast.88) | data formatting | bytes 8388608 | tf_op jit(solution)/shard_map/transpose | solution.py:46
  37.1 7.6 %reshape.148 = bf16[32,128,512]{2,1,0:T(8,128)(2,1)} reshape(bf16[4096,1,2,256]{3,2,0,1:T(2,128)(2,1)} %copy.64) | data formatting | bytes 8388608 | tf_op jit(solution)/shard_map/reshape | solution.py:46
  44.8 6.5 %copy.63 = bf16[1,2,4096,256]{2,3,1,0:T(8,128)(2,1)} copy(bf16[1,2,4096,256]{3,2,1,0:T(8,128)(2,1)} %param.16) | data formatting | bytes 8388608 | tf_op args[1]
  57.3 24.8 %all-to-all-done = bf16[1,1,2,1,128,32,256]{6,5,2,3,1,0,4:T(8,128)(2,1)} async-done(((bf16[1,1,2,1,128,32,256]{6,5,2,3,1,0,4:T(8,128)(2,1)}), bf16[1,1,2,1,128,32,256]{6,5,2,3,1,0,4:T(8,128)(2,1)}, u32[]{:S(2)}, u32[]{:S(2)}) %all-to-all-start) | async-done | bytes 4194336 | tf_op jit(solution)/shard_map/all_to_all | solution.py:41
  82.1 7.1 %copy.68 = bf16[8,1,2,1,32,16,256]{6,5,4,2,0,3,1:T(8,128)(2,1)} copy(bf16[8,1,2,1,32,16,256]{6,4,2,5,0,3,1:T(8,128)(2,1)} %bitcast.15) | data formatting | bytes 8388608 | tf_op jit(solution)/shard_map/transpose | solution.py:43
  89.2 7.2 %reshape_reshape.10 = bf16[8,2,1,32,32,128]{5,4,3,1,0,2:T(8,128)(2,1)} reshape(bf16[8,1,2,1,32,16,256]{6,5,4,2,0,3,1:T(8,128)(2,1)} %copy.68) | data formatting | bytes 8388608 | tf_op jit(solution)/shard_map/reshape;reshape | solution.py:62
  96.4 5.9 %copy.69 = bf16[2,32,1,8,32,128]{5,4,3,1,0,2:T(8,128)(2,1)} copy(bf16[2,32,1,8,32,128]{5,1,4,0,3,2:T(8,128)(2,1)} %bitcast.90) | data formatting | bytes 8388608 | tf_op jit(solution)/shard_map/transpose | solution.py:63
  102.3 10.7 %gather_fusion.3 = bf16[192,256,128]{2,1,0:T(8,128)(2,1)} fusion(bf16[64,1,256,128]{3,2,0,1:T(8,128)(2,1)} %bitcast.84, s32[192]{0:T(256)S(1)} %reshape.181), kind=kCustom, calls=%fused_computation.3 | custom fusion | bytes 25167360 | tf_op jit(solution)/shard_map/gather | solution.py:72
  112.9 13.7 %all-gather.5.cloned.1.call-done = bf16[256,128,128]{2,1,0:T(8,128)(2,1)} async-done(((bf16[16,128,128]{2,1,0:T(8,128)(2,1)}), bf16[256,128,128]{2,1,0:T(8,128)(2,1)}) %all-gather.5.cloned.1.call-update) | async-done | bytes 8388624 | tf_op jit(solution)/shard_map/all_gather | solution.py:36
  126.6 8.3 %gather_fusion.4 = bf16[48,4,128,128]{3,2,1,0:T(8,128)(2,1)} fusion(bf16[64,4,128,128]{3,2,1,0:T(8,128)(2,1)} %bitcast.93, s32[1024]{0:T(1024)S(1)} %pad_clamp_fusion.2), kind=kCustom, calls=%fused_computation.4 | custom fusion | bytes 12583104 | tf_op jit(solution)/shard_map/gather | solution.py:74
  134.9 13.0 %bitcast_select_fusion = f32[48,256,128]{2,1,0:T(8,128)} fusion(pred[48]{0:T(512)(128)(4,1)S(1)} %iota_compare_fusion.1, bf16[48,4,256,128]{3,2,1,0:T(8,128)(2,1)} %bitcast.92, bf16[48,4,128,128]{3,2,1,0:T(8,128)(2,1)} %gather_fusion.4), kind=kOutput, calls=%fused_computation.16 | convolution fusion | flops 1612185600 | bytes 25165872 | tf_op jit(solution)/shard_map/emrc,emcb->erb/dot_general | solution.py:73
  152.2 15.2 %scatter_fusion = f32[64,256,128]{2,1,0:T(8,128)} fusion(f32[64,256,128]{2,1,0:T(8,128)} %broadcast_in_dim.61, s32[48]{0:T(128)S(1)} %fusion.6, f32[48,256,128]{2,1,0:T(8,128)} %bitcast_select_fusion), kind=kCustom, calls=%fused_computation.5 | custom fusion | flops 1572864 | bytes 18874560 | tf_op jit(solution)/shard_map/scatter-add | solution.py:78
  176.4 7.2 %reshape_reshape.11 = bf16[8,1,2,1,32,16,256]{6,5,4,2,0,3,1:T(8,128)(2,1)} reshape(bf16[8,2,1,32,32,128]{5,4,3,1,0,2:T(8,128)(2,1)} %copy.71) | data formatting | bytes 8388608 | tf_op jit(solution)/shard_map/reshape;reshape | solution.py:87
  183.6 5.9 %copy.72 = bf16[8,16,1,2,1,32,256]{6,5,3,1,0,4,2:T(8,128)(2,1)} copy(bf16[8,16,1,2,1,32,256]{6,1,5,3,0,4,2:T(8,128)(2,1)} %bitcast.91) | data formatting | bytes 8388608 | tf_op jit(solution)/shard_map/transpose | solution.py:88
  189.4 8.8 %all-to-all-start.1 = ((bf16[128,1,2,1,1,32,256]{6,5,2,4,3,1,0:T(8,128)(2,1)}), bf16[128,1,2,1,1,32,256]{6,5,2,4,3,1,0:T(8,128)(2,1)}, u32[]{:S(2)}, u32[]{:S(2)}) async-start(bf16[128,1,2,1,1,32,256]{6,5,2,4,3,1,0:T(8,128)(2,1)} %bitcast.89), calls=%async_computation.1 | async-start | bytes 8388608 | tf_op jit(solution)/shard_map/all_to_all | solution.py:91
  199.3 83.7 %while.10 = (s32[]{:T(128)}, f32[4,8,128,512]{3,2,1,0:T(8,128)}, s32[4]{0:T(128)S(1)}, s32[32,8]{1,0:T(8,128)S(1)}, bf16[256,128,128]{2,1,0:T(8,128)(2,1)}, /*in...) while((s32[]{:T(128)}, f32[4,8,128,512]{3,2,1,0:T(8,128)}, ...), condition=%wide.region_1.2_spmd, body=%wide.region_0.1_spmd.sunk | while | flops 1073744256 | bytes 33566888 | solution.py:60
  206.5 7.7 %gather_fusion.1 = bf16[64,128,512]{2,1,0:T(8,128)(2,1)} fusion(bf16[32,128,512]{2,1,0:T(8,128)(2,1)} %get-tuple-element.168, s32[1024]{0:T(1024)S(1)} %pad_clamp_fusion.6), kind=kCustom, calls=%fused_computation.1.clone.1 | custom fusion | bytes 16777472 | tf_op jit(solution)/shard_map/while/body/eval_jaxpr/gather | solution.py:53
  214.2 6.0 %bitcast_dynamic-update-slice_fusion.2 = f32[4,8,128,512]{3,2,1,0:T(8,128)} fusion(f32[4,8,128,512]{3,2,1,0:T(8,128)} %get-tuple-element.153, s32[]{:T(128)S(6)} %copy.88, bf16[8,8,128,128]{3,2,1,0:T(8,128)(2,1)S(1)} %bitcast.83, bf16[8,8,128,512]{3,2,1,0:T(8,128)(2,1)} %bitcast.82), kind=kOutput, calls=%fused_computation.6.clone.1 | convolution fusion | flops 1073741824 | bytes 12582916 | tf_op jit(solution)/shard_map/while/body/eval_jaxpr/akrc,akce->are/dot_general | solution.py:55
  227.4 7.7 %gather_fusion.1 = bf16[64,128,512]{2,1,0:T(8,128)(2,1)} fusion(bf16[32,128,512]{2,1,0:T(8,128)(2,1)} %get-tuple-element.168, s32[1024]{0:T(1024)S(1)} %pad_clamp_fusion.6), kind=kCustom, calls=%fused_computation.1.clone.1 | custom fusion | bytes 16777472 | tf_op jit(solution)/shard_map/while/body/eval_jaxpr/gather | solution.py:53
  235.1 6.0 %bitcast_dynamic-update-slice_fusion.2 = f32[4,8,128,512]{3,2,1,0:T(8,128)} fusion(f32[4,8,128,512]{3,2,1,0:T(8,128)} %get-tuple-element.153, s32[]{:T(128)S(6)} %copy.88, bf16[8,8,128,128]{3,2,1,0:T(8,128)(2,1)S(1)} %bitcast.83, bf16[8,8,128,512]{3,2,1,0:T(8,128)(2,1)} %bitcast.82), kind=kOutput, calls=%fused_computation.6.clone.1 | convolution fusion | flops 1073741824 | bytes 12582916 | tf_op jit(solution)/shard_map/while/body/eval_jaxpr/akrc,akce->are/dot_general | solution.py:55
  248.3 7.7 %gather_fusion.1 = bf16[64,128,512]{2,1,0:T(8,128)(2,1)} fusion(bf16[32,128,512]{2,1,0:T(8,128)(2,1)} %get-tuple-element.168, s32[1024]{0:T(1024)S(1)} %pad_clamp_fusion.6), kind=kCustom, calls=%fused_computation.1.clone.1 | custom fusion | bytes 16777472 | tf_op jit(solution)/shard_map/while/body/eval_jaxpr/gather | solution.py:53
  256.0 6.0 %bitcast_dynamic-update-slice_fusion.2 = f32[4,8,128,512]{3,2,1,0:T(8,128)} fusion(f32[4,8,128,512]{3,2,1,0:T(8,128)} %get-tuple-element.153, s32[]{:T(128)S(6)} %copy.88, bf16[8,8,128,128]{3,2,1,0:T(8,128)(2,1)S(1)} %bitcast.83, bf16[8,8,128,512]{3,2,1,0:T(8,128)(2,1)} %bitcast.82), kind=kOutput, calls=%fused_computation.6.clone.1 | convolution fusion | flops 1073741824 | bytes 12582916 | tf_op jit(solution)/shard_map/while/body/eval_jaxpr/akrc,akce->are/dot_general | solution.py:55
  269.3 7.7 %gather_fusion.1 = bf16[64,128,512]{2,1,0:T(8,128)(2,1)} fusion(bf16[32,128,512]{2,1,0:T(8,128)(2,1)} %get-tuple-element.168, s32[1024]{0:T(1024)S(1)} %pad_clamp_fusion.6), kind=kCustom, calls=%fused_computation.1.clone.1 | custom fusion | bytes 16777472 | tf_op jit(solution)/shard_map/while/body/eval_jaxpr/gather | solution.py:53
  277.0 6.0 %bitcast_dynamic-update-slice_fusion.2 = f32[4,8,128,512]{3,2,1,0:T(8,128)} fusion(f32[4,8,128,512]{3,2,1,0:T(8,128)} %get-tuple-element.153, s32[]{:T(128)S(6)} %copy.88, bf16[8,8,128,128]{3,2,1,0:T(8,128)(2,1)S(1)} %bitcast.83, bf16[8,8,128,512]{3,2,1,0:T(8,128)(2,1)} %bitcast.82), kind=kOutput, calls=%fused_computation.6.clone.1 | convolution fusion | flops 1073741824 | bytes 12582916 | tf_op jit(solution)/shard_map/while/body/eval_jaxpr/akrc,akce->are/dot_general | solution.py:55
  283.0 10.5 %reshape.209 = f32[4096,1,2,256]{3,2,0,1:T(2,128)} reshape(f32[4,8,128,512]{3,2,1,0:T(8,128)} %get-tuple-element.42) | data formatting | bytes 16777216 | tf_op jit(solution)/shard_map/reshape | solution.py:61
  293.5 13.1 %copy.79 = f32[4096,1,2,256]{0,3,2,1:T(8,128)} copy(f32[4096,1,2,256]{3,2,0,1:T(2,128)} %reshape.209) | data formatting | bytes 16777216 | tf_op jit(solution)/shard_map/reshape | solution.py:61
  306.6 6.5 %bitcast_convert_fusion = f32[128,1,1,2,1,1,32,256]{7,6,0,3,5,4,2,1:T(8,128)} fusion(bf16[128,1,2,1,1,32,256]{6,5,2,4,3,1,0:T(8,128)(2,1)} %all-to-all-done.1), kind=kLoop, calls=%fused_computation.17 | loop fusion | flops 2097152 | bytes 12582912 | tf_op jit(solution)/shard_map/convert_element_type | solution.py:109
  313.1 9.0 %copy.75 = f32[1,2,4096,256]{2,3,1,0:T(8,128)} copy(f32[1,2,4096,256]{3,2,1,0:T(8,128)} %bitcast.85) | data formatting | bytes 16777216 | tf_op jit(solution)/shard_map/convert_element_type | solution.py:109
  322.1 11.7 %fusion.2 = bf16[1,2,4096,256]{2,3,1,0:T(8,128)(2,1)} fusion(f32[1,2,4096,256]{2,3,1,0:T(8,128)} %copy.75, f32[4096,1,2,256]{0,3,2,1:T(8,128)} %copy.79, bf16[1,2,4096,256]{2,3,1,0:T(8,128)(2,1)} %copy.63, f32[2]{0:T(128)S(1)} %fusion.5, f32[4096,256]{0,1:T(8,128)} %add_subtract_fusion), kind=kLoop, calls=%fused_computation.15 | loop fusion | flops 12582912 | bytes 29360136 | tf_op jit(solution)/shard_map/convert_element_type | solution.py:110
  333.8 6.3 %copy.76 = bf16[1,2,4096,256]{3,2,1,0:T(8,128)(2,1)} copy(bf16[1,2,4096,256]{2,3,1,0:T(8,128)(2,1)} %fusion.2) | data formatting | bytes 8388608 | tf_op jit(solution)/shard_map/convert_element_type | solution.py:110
  (81 shorter events, 45.0 us)
Async XLA Ops:
  6.5 120.1 %all-gather.5.cloned.1.call-start = ((), (), s32[]{:S(2)}) async-start(), calls=%async_computation.3 | async-start | bytes 8912896 | tf_op jit(solution)/shard_map/all_gather | solution.py:36
  7.3 192.0 %all-gather.3.cloned.1.call-start = ((), (), s32[]{:S(2)}) async-start(), calls=%async_computation.2 | async-start | bytes 8912896 | tf_op jit(solution)/shard_map/all_gather | solution.py:35
  12.9 12.0 %copy-start.3 = (s32[64,4]{0,1:T(4,128)S(1)}, s32[64,4]{0,1:T(4,128)}, u32[]{:S(2)}) copy-start(s32[64,4]{0,1:T(4,128)} %param.21) | copy-start | bytes 3076
  12.9 12.1 %copy-start.6 = (s32[32]{0:T(128)S(1)}, s32[32]{0:T(128)}, u32[]{:S(2)}) copy-start(s32[32]{0:T(128)} %param.23) | copy-start | bytes 388
  12.9 14.1 %copy-start.4 = (s32[256]{0:T(256)S(1)}, s32[256]{0:T(256)}, u32[]{:S(2)}) copy-start(s32[256]{0:T(256)} %param.20) | copy-start | bytes 3076
  12.9 69.2 %all-to-all-start = ((bf16[1,1,2,1,128,32,256]{6,5,2,3,1,0,4:T(8,128)(2,1)}), bf16[1,1,2,1,128,32,256]{6,5,2,3,1,0,4:T(8,128)(2,1)}, u32[]{:S(2)}, u32[]{:S(2)}) async-start(bf16[1,1,2,1,128,32,256]{6,5,2,3,1,0,4:T(8,128)(2,1)} %copy.67), calls=%async_computation | async-start | bytes 8388608 | tf_op jit(solution)/shard_map/all_to_all | solution.py:41
  44.7 6.5 %copy-start.7 = (s32[8]{0:T(128)S(1)}, s32[8]{0:T(128)}, u32[]{:S(2)}) copy-start(s32[8]{0:T(128)} %param.24) | copy-start | bytes 100
  44.7 7.2 %copy-start.1 = (f32[4096]{0:T(1024)S(1)}, f32[4096]{0:T(1024)}, u32[]{:S(2)}) copy-start(f32[4096]{0:T(1024)} %param.27) | copy-start | bytes 49156
  44.7 7.9 %copy-start.2 = (f32[400]{0:T(512)S(1)}, f32[400]{0:T(512)}, u32[]{:S(2)}) copy-start(f32[400]{0:T(512)} %param.26) | copy-start | bytes 4804
  44.7 9.2 %copy-start.5 = (s32[2]{0:T(128)S(1)}, s32[2]{0:T(128)}, u32[]{:S(2)}) copy-start(s32[2]{0:T(128)} %param.25) | copy-start | bytes 28
  189.4 9.9 %copy-start = (s32[32,8]{0,1:T(8,128)S(1)}, s32[32,8]{0,1:T(8,128)}, u32[]{:S(2)}) copy-start(s32[32,8]{0,1:T(8,128)} %param.19) | copy-start | bytes 3076
  189.4 117.2 %all-to-all-start.1 = ((bf16[128,1,2,1,1,32,256]{6,5,2,4,3,1,0:T(8,128)(2,1)}), bf16[128,1,2,1,1,32,256]{6,5,2,4,3,1,0:T(8,128)(2,1)}, u32[]{:S(2)}, u32[]{:S(2)}) async-start(bf16[128,1,2,1,1,32,256]{6,5,2,4,3,1,0:T(8,128)(2,1)} %bitcast.89), calls=%async_computation.1 | async-start | bytes 8388608 | tf_op jit(solution)/shard_map/all_to_all | solution.py:91
Sparse Core Ops, SparseCore 0:
  9.5 117.1 all-gather.4
  128.8 70.4 all-gather.2
where the time goes:
time: 350 us; the launch traced here: 347 us
  local copies, waits for them, and re-layouts  183 us (52%)
  other arithmetic  43.8 us (13%)
  waiting for transfers between devices  40.9 us (12%)
  matrix products  36.9 us (11%)
  starting transfers between devices  20.8 us (6%)
  between operations  13.5 us (4%)
  loops' own time  7.72 us (2%)
    gather x4, local copies, waits for them, and re-layouts, ladder_block(): picked_rows = arranged[screen_part]  30.8 us
    all_to_all x1, waiting for transfers between devices, body(): lax.all_to_all(flat, ('occ', 'vir'), split_axis=4, concat_axis=0, tiled=T...  24.8 us
    dot_general x4, matrix products, ladder_block(): jnp.einsum('akrc,akce->are', weights, picked_rows, preferred_element_type...  24 us
    reshape x2, local copies, waits for them, and re-layouts, body(): total.reshape(width_all, slab_rows, window, block_cols)  23.7 us
    gather x4, local copies, waits for them, and re-layouts, ladder_block(): weights = all_ladder[slot_part]  17.3 us
    scatter-add x1, other arithmetic, body(): jnp.zeros((column_tiles, slab_all * inner, tile_side), jnp.float32)  15.2 us
    all_gather x1, waiting for transfers between devices, body(): lax.all_gather(cycle_tiles, 'vir', axis=0, tiled=True)  13.7 us
    dot_general x1, matrix products, body(): jnp.einsum('emrc,emcb->erb', picked, cycle_sel[columns], preferred_elemen...  13 us
  transfers between devices with their start and end apart: 4, of which 3 were waited for; matrix products, arithmetic and copies ran while one was open for 66% of the time, Pallas kernels for 0%

commit v1 on v0

--- a/solution.py
+++ b/solution.py
@@ -33,7 +33,9 @@
     slab_all = slab_rows * occ_count
     all_ladder, all_cycle = (
         lax.all_gather(ladder_tiles, "vir", axis=0, tiled=True),
-        lax.all_gather(cycle_tiles, "vir", axis=0, tiled=True),
+        jnp.concatenate(
+            lax.all_to_all(jnp.stack([cycle_tiles] * lax.axis_size("vir")), "vir", 0, 0), axis=0
+        ),
     )
     front, inner = (1, rows_here)
     split = amplitudes.reshape(slab_rows, window, front, occ_count, vir_count, inner, block_cols)

time: 350 us -> 543 us (1.55)
  waiting for transfers between devices: 40.9 us -> 207 us
  starting transfers between devices: 20.8 us -> 42.9 us
  local copies, waits for them, and re-layouts: 183 us -> 189 us
    all_to_all x0 -> x1, waiting for transfers between devices: none -> 132 us  [body(): lax.all_to_all(jnp.stack([cycle_tiles] * lax.axis_size('vir')), 'vir', 0, 0)]
    all_to_all x1, waiting for transfers between devices: 24.8 us -> 52.3 us  [body(): lax.all_to_all(flat, ('occ', 'vir'), split_axis=4, concat_axis=0, tiled=T...]
    all_to_all x1, waiting for transfers between devices: 0.01 us -> 22.2 us  [body(): lax.all_to_all(shaped, ('occ', 'vir'), split_axis=0, concat_axis=4, tiled...]
    all_to_all x1, starting transfers between devices: 8.83 us -> 24 us  [body(): lax.all_to_all(shaped, ('occ', 'vir'), split_axis=0, concat_axis=4, tiled...]
    all_gather x1 -> x0, waiting for transfers between devices: 13.7 us -> none  [body(): lax.all_gather(cycle_tiles, 'vir', axis=0, tiled=True)]
    all_to_all x0 -> x1, starting transfers between devices: none -> 6.88 us  [body(): lax.all_to_all(jnp.stack([cycle_tiles] * lax.axis_size('vir')), 'vir', 0, 0)]
    another operation x0 -> x1, local copies, waits for them, and re-layouts: none -> 5.47 us  [body(): jnp.stack([cycle_tiles] * lax.axis_size('vir'))]
  transfers between devices with their start and end apart: 4 -> 4, of which waited for: 3 -> 3; matrix products, arithmetic and copies ran while one was open for 66% -> 27% of each run, Pallas kernels for 0% -> 0%
where the time goes in v1:
time: 543 us; the launch traced here: 540 us
  waiting for transfers between devices  207 us (38%)
  local copies, waits for them, and re-layouts  189 us (35%)
  other arithmetic  43.7 us (8%)
  starting transfers between devices  42.9 us (8%)
  matrix products  36.4 us (7%)
  between operations  13.5 us (2%)
  loops' own time  7.86 us (1%)
    all_to_all x1, waiting for transfers between devices, body(): lax.all_to_all(jnp.stack([cycle_tiles] * lax.axis_size('vir')), 'vir', 0, 0)  132 us
    all_to_all x1, waiting for transfers between devices, body(): lax.all_to_all(flat, ('occ', 'vir'), split_axis=4, concat_axis=0, tiled=T...  52.3 us
    gather x4, local copies, waits for them, and re-layouts, ladder_block(): picked_rows = arranged[screen_part]  31.3 us
    all_to_all x1, starting transfers between devices, body(): lax.all_to_all(shaped, ('occ', 'vir'), split_axis=0, concat_axis=4, tiled...  24 us
    dot_general x4, matrix products, ladder_block(): jnp.einsum('akrc,akce->are', weights, picked_rows, preferred_element_type...  24 us
    reshape x2, local copies, waits for them, and re-layouts, body(): total.reshape(width_all, slab_rows, window, block_cols)  23.7 us
    all_to_all x1, waiting for transfers between devices, body(): lax.all_to_all(shaped, ('occ', 'vir'), split_axis=0, concat_axis=4, tiled...  22.2 us
    gather x4, local copies, waits for them, and re-layouts, ladder_block(): weights = all_ladder[slot_part]  17.3 us
  transfers between devices with their start and end apart: 4, of which 3 were waited for; matrix products, arithmetic and copies ran while one was open for 27% of the time, Pallas kernels for 0%

profile of v1, /device:TPU:1, one launch (start us, length us, event | category | flops | bytes accessed | tf_op | source)
XLA Modules:
  0.0 540.0 jit_solution(14434707343452534979)
XLA Ops:
  11.4 11.9 %all-to-all-start = ((bf16[1,1,2,1,128,32,256]{6,5,2,3,1,0,4:T(8,128)(2,1)}), bf16[1,1,2,1,128,32,256]{6,5,2,3,1,0,4:T(8,128)(2,1)}, u32[]{:S(2)}, u32[]{:S(2)}) async-start(bf16[1,1,2,1,128,32,256]{6,5,2,3,1,0,4:T(8,128)(2,1)} %copy.67), calls=%async_computation | async-start | bytes 8388608 | tf_op jit(solution)/shard_map/all_to_all | solution.py:43
  24.1 52.3 %all-to-all-done = bf16[1,1,2,1,128,32,256]{6,5,2,3,1,0,4:T(8,128)(2,1)} async-done(((bf16[1,1,2,1,128,32,256]{6,5,2,3,1,0,4:T(8,128)(2,1)}), bf16[1,1,2,1,128,32,256]{6,5,2,3,1,0,4:T(8,128)(2,1)}, u32[]{:S(2)}, u32[]{:S(2)}) %all-to-all-start) | async-done | bytes 4194336 | tf_op jit(solution)/shard_map/all_to_all | solution.py:43
  81.8 6.9 %all-to-all-start.1 = ((bf16[16,16,128,128]{3,2,1,0:T(8,128)(2,1)}), bf16[16,16,128,128]{3,2,1,0:T(8,128)(2,1)}, u32[]{:S(2)}, u32[]{:S(2)}) async-start(bf16[16,16,128,128]{3,2,1,0:T(8,128)(2,1)} %stack.2), calls=%async_computation.1 | async-start | bytes 16777216 | tf_op jit(solution)/shard_map/all_to_all | solution.py:37
  91.5 7.1 %copy.68 = bf16[8,1,2,1,32,16,256]{6,5,4,2,0,3,1:T(8,128)(2,1)} copy(bf16[8,1,2,1,32,16,256]{6,4,2,5,0,3,1:T(8,128)(2,1)} %bitcast.15) | data formatting | bytes 8388608 | tf_op jit(solution)/shard_map/transpose | solution.py:45
  98.6 7.1 %reshape_reshape.13 = bf16[8,2,1,32,32,128]{5,4,3,1,0,2:T(8,128)(2,1)} reshape(bf16[8,1,2,1,32,16,256]{6,5,4,2,0,3,1:T(8,128)(2,1)} %copy.68) | data formatting | bytes 8388608 | tf_op jit(solution)/shard_map/reshape;reshape | solution.py:64
  111.5 10.6 %gather_fusion.3 = bf16[192,256,128]{2,1,0:T(8,128)(2,1)} fusion(bf16[64,1,256,128]{3,2,0,1:T(8,128)(2,1)} %bitcast.84, s32[192]{0:T(256)S(1)} %reshape.179), kind=kCustom, calls=%fused_computation.3 | custom fusion | bytes 25167360 | tf_op jit(solution)/shard_map/gather | solution.py:74
  122.1 131.5 %all-to-all-done.1 = bf16[16,16,128,128]{3,2,1,0:T(8,128)(2,1)} async-done(((bf16[16,16,128,128]{3,2,1,0:T(8,128)(2,1)}), bf16[16,16,128,128]{3,2,1,0:T(8,128)(2,1)}, u32[]{:S(2)}, u32[]{:S(2)}) %all-to-all-start.1) | async-done | bytes 8388640 | tf_op jit(solution)/shard_map/all_to_all | solution.py:37
  253.7 8.3 %gather_fusion.4 = bf16[48,4,128,128]{3,2,1,0:T(8,128)(2,1)} fusion(bf16[64,4,128,128]{3,2,1,0:T(8,128)(2,1)} %bitcast.20, s32[1024]{0:T(1024)S(1)} %pad_clamp_fusion.2), kind=kCustom, calls=%fused_computation.4 | custom fusion | bytes 12583104 | tf_op jit(solution)/shard_map/gather | solution.py:76
  262.0 12.4 %bitcast_select_fusion = f32[48,256,128]{2,1,0:T(8,128)} fusion(pred[48]{0:T(512)(128)(4,1)S(1)} %iota_compare_fusion.1, bf16[48,4,256,128]{3,2,1,0:T(8,128)(2,1)} %bitcast.92, bf16[48,4,128,128]{3,2,1,0:T(8,128)(2,1)} %gather_fusion.4), kind=kOutput, calls=%fused_computation.16 | convolution fusion | flops 1612185600 | bytes 25165872 | tf_op jit(solution)/shard_map/emrc,emcb->erb/dot_general | solution.py:75
  278.7 15.2 %scatter_fusion = f32[64,256,128]{2,1,0:T(8,128)} fusion(f32[64,256,128]{2,1,0:T(8,128)} %broadcast_in_dim.61, s32[48]{0:T(128)S(1)} %fusion.6, f32[48,256,128]{2,1,0:T(8,128)} %bitcast_select_fusion), kind=kCustom, calls=%fused_computation.5 | custom fusion | flops 1572864 | bytes 18874560 | tf_op jit(solution)/shard_map/scatter-add | solution.py:80
  302.7 7.1 %reshape_reshape.15 = bf16[8,1,2,1,32,16,256]{6,5,4,2,0,3,1:T(8,128)(2,1)} reshape(bf16[8,2,1,32,32,128]{5,4,3,1,0,2:T(8,128)(2,1)} %copy.71) | data formatting | bytes 8388608 | tf_op jit(solution)/shard_map/reshape;reshape | solution.py:89
  309.8 5.8 %copy.72 = bf16[8,16,1,2,1,32,256]{6,5,3,1,0,4,2:T(8,128)(2,1)} copy(bf16[8,16,1,2,1,32,256]{6,1,5,3,0,4,2:T(8,128)(2,1)} %bitcast.91) | data formatting | bytes 8388608 | tf_op jit(solution)/shard_map/transpose | solution.py:90
  315.7 24.0 %all-to-all-start.2 = ((bf16[128,1,2,1,1,32,256]{6,5,2,4,3,1,0:T(8,128)(2,1)}), bf16[128,1,2,1,1,32,256]{6,5,2,4,3,1,0:T(8,128)(2,1)}, u32[]{:S(2)}, u32[]{:S(2)}) async-start(bf16[128,1,2,1,1,32,256]{6,5,2,4,3,1,0:T(8,128)(2,1)} %bitcast.89), calls=%async_computation.2 | async-start | bytes 8388608 | tf_op jit(solution)/shard_map/all_to_all | solution.py:93
  339.8 10.2 %copy.64 = bf16[4096,1,2,256]{3,2,0,1:T(2,128)(2,1)} copy(bf16[4096,1,2,256]{3,0,2,1:T(8,128)(2,1)} %bitcast.88) | data formatting | bytes 8388608 | tf_op jit(solution)/shard_map/transpose | solution.py:48
  349.9 7.7 %reshape.147 = bf16[32,128,512]{2,1,0:T(8,128)(2,1)} reshape(bf16[4096,1,2,256]{3,2,0,1:T(2,128)(2,1)} %copy.64) | data formatting | bytes 8388608 | tf_op jit(solution)/shard_map/reshape | solution.py:48
  357.6 6.5 %copy.63 = bf16[1,2,4096,256]{2,3,1,0:T(8,128)(2,1)} copy(bf16[1,2,4096,256]{3,2,1,0:T(8,128)(2,1)} %param.16) | data formatting | bytes 8388608 | tf_op args[1]
  369.3 22.2 %all-to-all-done.2 = bf16[128,1,2,1,1,32,256]{6,5,2,4,3,1,0:T(8,128)(2,1)} async-done(((bf16[128,1,2,1,1,32,256]{6,5,2,4,3,1,0:T(8,128)(2,1)}), bf16[128,1,2,1,1,32,256]{6,5,2,4,3,1,0:T(8,128)(2,1)}, u32[]{:S(2)}, u32[]{:S(2)}) %all-to-all-start.2) | async-done | bytes 4194336 | tf_op jit(solution)/shard_map/all_to_all | solution.py:93
  391.6 6.6 %bitcast_convert_fusion = f32[128,1,1,2,1,1,32,256]{7,6,0,3,5,4,2,1:T(8,128)} fusion(bf16[128,1,2,1,1,32,256]{6,5,2,4,3,1,0:T(8,128)(2,1)} %all-to-all-done.2), kind=kLoop, calls=%fused_computation.17 | loop fusion | flops 2097152 | bytes 12582912 | tf_op jit(solution)/shard_map/convert_element_type | solution.py:111
  398.2 9.0 %copy.75 = f32[1,2,4096,256]{2,3,1,0:T(8,128)} copy(f32[1,2,4096,256]{3,2,1,0:T(8,128)} %bitcast.85) | data formatting | bytes 16777216 | tf_op jit(solution)/shard_map/convert_element_type | solution.py:111
  407.2 84.2 %while.10 = (s32[]{:T(128)}, f32[4,8,128,512]{3,2,1,0:T(8,128)}, s32[4]{0:T(128)S(1)}, s32[32,8]{1,0:T(8,128)S(1)}, bf16[256,128,128]{2,1,0:T(8,128)(2,1)}, /*in...) while((s32[]{:T(128)}, f32[4,8,128,512]{3,2,1,0:T(8,128)}, ...), condition=%wide.region_1.2_spmd, body=%wide.region_0.1_spmd.sunk | while | flops 1073744256 | bytes 33566888 | solution.py:62
  414.4 7.8 %gather_fusion.1 = bf16[64,128,512]{2,1,0:T(8,128)(2,1)} fusion(bf16[32,128,512]{2,1,0:T(8,128)(2,1)} %get-tuple-element.168, s32[1024]{0:T(1024)S(1)} %pad_clamp_fusion.6), kind=kCustom, calls=%fused_computation.1.clone.1 | custom fusion | bytes 16777472 | tf_op jit(solution)/shard_map/while/body/eval_jaxpr/gather | solution.py:55
  422.2 6.0 %bitcast_dynamic-update-slice_fusion.2 = f32[4,8,128,512]{3,2,1,0:T(8,128)} fusion(f32[4,8,128,512]{3,2,1,0:T(8,128)} %get-tuple-element.153, s32[]{:T(128)S(6)} %copy.88, bf16[8,8,128,128]{3,2,1,0:T(8,128)(2,1)S(1)} %bitcast.83, bf16[8,8,128,512]{3,2,1,0:T(8,128)(2,1)} %bitcast.82), kind=kOutput, calls=%fused_computation.6.clone.1 | convolution fusion | flops 1073741824 | bytes 12582916 | tf_op jit(solution)/shard_map/while/body/eval_jaxpr/akrc,akce->are/dot_general | solution.py:57
  435.5 7.8 %gather_fusion.1 = bf16[64,128,512]{2,1,0:T(8,128)(2,1)} fusion(bf16[32,128,512]{2,1,0:T(8,128)(2,1)} %get-tuple-element.168, s32[1024]{0:T(1024)S(1)} %pad_clamp_fusion.6), kind=kCustom, calls=%fused_computation.1.clone.1 | custom fusion | bytes 16777472 | tf_op jit(solution)/shard_map/while/body/eval_jaxpr/gather | solution.py:55
  443.3 6.0 %bitcast_dynamic-update-slice_fusion.2 = f32[4,8,128,512]{3,2,1,0:T(8,128)} fusion(f32[4,8,128,512]{3,2,1,0:T(8,128)} %get-tuple-element.153, s32[]{:T(128)S(6)} %copy.88, bf16[8,8,128,128]{3,2,1,0:T(8,128)(2,1)S(1)} %bitcast.83, bf16[8,8,128,512]{3,2,1,0:T(8,128)(2,1)} %bitcast.82), kind=kOutput, calls=%fused_computation.6.clone.1 | convolution fusion | flops 1073741824 | bytes 12582916 | tf_op jit(solution)/shard_map/while/body/eval_jaxpr/akrc,akce->are/dot_general | solution.py:57
  456.5 7.8 %gather_fusion.1 = bf16[64,128,512]{2,1,0:T(8,128)(2,1)} fusion(bf16[32,128,512]{2,1,0:T(8,128)(2,1)} %get-tuple-element.168, s32[1024]{0:T(1024)S(1)} %pad_clamp_fusion.6), kind=kCustom, calls=%fused_computation.1.clone.1 | custom fusion | bytes 16777472 | tf_op jit(solution)/shard_map/while/body/eval_jaxpr/gather | solution.py:55
  464.3 6.0 %bitcast_dynamic-update-slice_fusion.2 = f32[4,8,128,512]{3,2,1,0:T(8,128)} fusion(f32[4,8,128,512]{3,2,1,0:T(8,128)} %get-tuple-element.153, s32[]{:T(128)S(6)} %copy.88, bf16[8,8,128,128]{3,2,1,0:T(8,128)(2,1)S(1)} %bitcast.83, bf16[8,8,128,512]{3,2,1,0:T(8,128)(2,1)} %bitcast.82), kind=kOutput, calls=%fused_computation.6.clone.1 | convolution fusion | flops 1073741824 | bytes 12582916 | tf_op jit(solution)/shard_map/while/body/eval_jaxpr/akrc,akce->are/dot_general | solution.py:57
  477.6 7.9 %gather_fusion.1 = bf16[64,128,512]{2,1,0:T(8,128)(2,1)} fusion(bf16[32,128,512]{2,1,0:T(8,128)(2,1)} %get-tuple-element.168, s32[1024]{0:T(1024)S(1)} %pad_clamp_fusion.6), kind=kCustom, calls=%fused_computation.1.clone.1 | custom fusion | bytes 16777472 | tf_op jit(solution)/shard_map/while/body/eval_jaxpr/gather | solution.py:55
  485.4 6.0 %bitcast_dynamic-update-slice_fusion.2 = f32[4,8,128,512]{3,2,1,0:T(8,128)} fusion(f32[4,8,128,512]{3,2,1,0:T(8,128)} %get-tuple-element.153, s32[]{:T(128)S(6)} %copy.88, bf16[8,8,128,128]{3,2,1,0:T(8,128)(2,1)S(1)} %bitcast.83, bf16[8,8,128,512]{3,2,1,0:T(8,128)(2,1)} %bitcast.82), kind=kOutput, calls=%fused_computation.6.clone.1 | convolution fusion | flops 1073741824 | bytes 12582916 | tf_op jit(solution)/shard_map/while/body/eval_jaxpr/akrc,akce->are/dot_general | solution.py:57
  491.4 10.6 %reshape.207 = f32[4096,1,2,256]{3,2,0,1:T(2,128)} reshape(f32[4,8,128,512]{3,2,1,0:T(8,128)} %get-tuple-element.42) | data formatting | bytes 16777216 | tf_op jit(solution)/shard_map/reshape | solution.py:63
  502.0 13.2 %copy.79 = f32[4096,1,2,256]{0,3,2,1:T(8,128)} copy(f32[4096,1,2,256]{3,2,0,1:T(2,128)} %reshape.207) | data formatting | bytes 16777216 | tf_op jit(solution)/shard_map/reshape | solution.py:63
  515.2 11.6 %fusion.2 = bf16[1,2,4096,256]{2,3,1,0:T(8,128)(2,1)} fusion(f32[1,2,4096,256]{2,3,1,0:T(8,128)} %copy.75, f32[4096,1,2,256]{0,3,2,1:T(8,128)} %copy.79, bf16[1,2,4096,256]{2,3,1,0:T(8,128)(2,1)} %copy.63, f32[2]{0:T(128)S(1)} %fusion.5, f32[4096,256]{0,1:T(8,128)} %add_subtract_fusion), kind=kLoop, calls=%fused_computation.15 | loop fusion | flops 12582912 | bytes 29360136 | tf_op jit(solution)/shard_map/convert_element_type | solution.py:112
  526.8 6.3 %copy.76 = bf16[1,2,4096,256]{3,2,1,0:T(8,128)(2,1)} copy(bf16[1,2,4096,256]{2,3,1,0:T(8,128)(2,1)} %fusion.2) | data formatting | bytes 8388608 | tf_op jit(solution)/shard_map/convert_element_type | solution.py:112
  (83 shorter events, 59.1 us)
Async XLA Ops:
  11.4 65.0 %copy-start = (bf16[16,128,128]{2,1,0:T(8,128)(2,1)S(1)}, bf16[16,128,128]{2,1,0:T(8,128)(2,1)}, u32[]{:S(2)}) copy-start(bf16[16,128,128]{2,1,0:T(8,128)(2,1)} %param.18) | copy-start | bytes 1572868
  11.4 65.0 %all-to-all-start = ((bf16[1,1,2,1,128,32,256]{6,5,2,3,1,0,4:T(8,128)(2,1)}), bf16[1,1,2,1,128,32,256]{6,5,2,3,1,0,4:T(8,128)(2,1)}, u32[]{:S(2)}, u32[]{:S(2)}) async-start(bf16[1,1,2,1,128,32,256]{6,5,2,3,1,0,4:T(8,128)(2,1)} %copy.67), calls=%async_computation | async-start | bytes 8388608 | tf_op jit(solution)/shard_map/all_to_all | solution.py:43
  23.3 383.8 %all-gather.2.cloned.1.call-start = ((), (), s32[]{:S(2)}) async-start(), calls=%async_computation.3 | async-start | bytes 8912896 | tf_op jit(solution)/shard_map/all_gather | solution.py:35
  81.8 6.9 %copy-start.4 = (s32[64,4]{0,1:T(4,128)S(1)}, s32[64,4]{0,1:T(4,128)}, u32[]{:S(2)}) copy-start(s32[64,4]{0,1:T(4,128)} %param.21) | copy-start | bytes 3076
  81.8 7.0 %copy-start.7 = (s32[32]{0:T(128)S(1)}, s32[32]{0:T(128)}, u32[]{:S(2)}) copy-start(s32[32]{0:T(128)} %param.23) | copy-start | bytes 388
  81.8 171.8 %all-to-all-start.1 = ((bf16[16,16,128,128]{3,2,1,0:T(8,128)(2,1)}), bf16[16,16,128,128]{3,2,1,0:T(8,128)(2,1)}, u32[]{:S(2)}, u32[]{:S(2)}) async-start(bf16[16,16,128,128]{3,2,1,0:T(8,128)(2,1)} %stack.2), calls=%async_computation.1 | async-start | bytes 16777216 | tf_op jit(solution)/shard_map/all_to_all | solution.py:37
  315.7 24.0 %copy-start.5 = (s32[256]{0:T(256)S(1)}, s32[256]{0:T(256)}, u32[]{:S(2)}) copy-start(s32[256]{0:T(256)} %param.20) | copy-start | bytes 3076
  315.7 75.9 %all-to-all-start.2 = ((bf16[128,1,2,1,1,32,256]{6,5,2,4,3,1,0:T(8,128)(2,1)}), bf16[128,1,2,1,1,32,256]{6,5,2,4,3,1,0:T(8,128)(2,1)}, u32[]{:S(2)}, u32[]{:S(2)}) async-start(bf16[128,1,2,1,1,32,256]{6,5,2,4,3,1,0:T(8,128)(2,1)} %bitcast.89), calls=%async_computation.2 | async-start | bytes 8388608 | tf_op jit(solution)/shard_map/all_to_all | solution.py:93
  357.6 6.5 %copy-start.8 = (s32[8]{0:T(128)S(1)}, s32[8]{0:T(128)}, u32[]{:S(2)}) copy-start(s32[8]{0:T(128)} %param.24) | copy-start | bytes 100
  357.6 7.1 %copy-start.2 = (f32[4096]{0:T(1024)S(1)}, f32[4096]{0:T(1024)}, u32[]{:S(2)}) copy-start(f32[4096]{0:T(1024)} %param.27) | copy-start | bytes 49156
  357.6 7.2 %copy-start.3 = (f32[400]{0:T(512)S(1)}, f32[400]{0:T(512)}, u32[]{:S(2)}) copy-start(f32[400]{0:T(512)} %param.26) | copy-start | bytes 4804
  357.6 8.4 %copy-start.6 = (s32[2]{0:T(128)S(1)}, s32[2]{0:T(128)}, u32[]{:S(2)}) copy-start(s32[2]{0:T(128)} %param.25) | copy-start | bytes 28
  398.2 9.0 %copy-start.1 = (s32[32,8]{0,1:T(8,128)S(1)}, s32[32,8]{0,1:T(8,128)}, u32[]{:S(2)}) copy-start(s32[32,8]{0,1:T(8,128)} %param.19) | copy-start | bytes 3076
Sparse Core Ops, SparseCore 0:
  26.3 193.0 all-gather.1
